TPU v7x, 32 devices: a whole 2x2x4 slice. The times are simulated.
32 devices in a mesh: groups: 2 (over y), seq: 16 (over z, x, core).
Axes of the slice: x: 2, y: 2, z: 4, core: 2. Of those that a mesh axis runs over, the one named last changes fastest.
Arguments:
- tokens: bfloat16 [4096, 256], P(('groups', 'seq')), parts along dimension 0, may hold values from -6 to 6
- inv_rms_a: float32 [4096], P(('groups', 'seq')), parts along dimension 0, may hold values from 0.5 to 2
- gain_a: float32 [256], replicated, may hold values from 0.1 to 1.9
- proj_a: bfloat16 [256, 768], replicated, may hold values from -0.375 to 0.375
- taps_a: bfloat16 [128, 256], replicated, may hold values from -0.5 to 0.5
- out_a: bfloat16 [256, 256], replicated, may hold values from -0.375 to 0.375
- inv_rms_b: float32 [4096], P(('groups', 'seq')), parts along dimension 0, may hold values from 0.5 to 2
- gain_b: float32 [256], replicated, may hold values from 0.1 to 1.9
- proj_b: bfloat16 [256, 768], replicated, may hold values from -0.375 to 0.375
- rates_b: float32 [16, 256], replicated, may hold values from 1.4648438e-06 to 0.033
- residues_b: float32 [16, 256], replicated, may hold values from -4 to 4
- out_b: bfloat16 [256, 256], replicated, may hold values from -0.375 to 0.375
Outputs:
- partial_a: bfloat16 [4096, 256], P(('groups', 'seq')), parts along dimension 0
- partial_b: bfloat16 [4096, 256], P(('groups', 'seq')), parts along dimension 0
There are 2 independent parts, one for each index of `groups`. A program takes and returns all parts, laid end to end along the dimension named above; an argument that names none is the same for every part. Nothing has to cross between parts.
All inputs are finite; a program needn't handle non-finite values.
Results may differ from a plain program's by a relative error of at most 0.019.
Values may be sent and summed in bfloat16 or wider, within the bound.
A program may use at most 64 MiB of HBM per device.

v0:
```python
import functools

import jax
import jax.numpy as jnp
import numpy as np
from jax import lax
from jax.experimental import pallas as pl
from jax.experimental.pallas import tpu as pltpu
from jax.sharding import PartitionSpec as P

MESH = pl.DeviceIdType.MESH
F32 = jnp.float32
BF16 = jnp.bfloat16
SUB = 8
LANES = 128


def dft_tables(rows):
    freq = (np.arange(rows) + 0.5)[:, None]
    angle = freq * np.arange(rows)[None, :] * (np.pi / rows)
    cos, sin = np.cos(angle), np.sin(angle)
    sign = np.where(np.arange(rows) % 2 == 0, 1.0, -1.0)[:, None]
    own = np.concatenate([cos, sin], 0)
    behind = np.concatenate([sign * sin, -sign * cos], 0)
    back = own.T / rows
    return [jnp.asarray(t, F32).astype(BF16) for t in (own, behind, back)]


def dot(left, right):
    return jnp.dot(left, right, preferred_element_type=F32)


def split(value):
    high = value.astype(BF16)
    return high, (value - high.astype(F32)).astype(BF16)


def one_minus_exp(a):
    series = 1.0 - a / 9.0
    for k in (8.0, 7.0, 6.0, 5.0, 4.0, 3.0, 2.0):
        series = 1.0 - series * a / k
    return jnp.where(a < 0.5, a * series, 1.0 - jnp.exp(-a))


def column(row):
    rows = row.shape[1]
    eye = lax.broadcasted_iota(jnp.int32, (rows, rows), 0) == lax.broadcasted_iota(
        jnp.int32, (rows, rows), 1
    )
    return jnp.sum(jnp.where(eye, row, 0.0), axis=1, keepdims=True)


def scaled(tokens, scale, gain):
    return (tokens.astype(F32) * scale * gain).astype(BF16)


def spectral_product(data, filt):
    half = data.shape[0] // 2
    dc, ds, fc, fs = data[:half], data[half:], filt[:half], filt[half:]
    return jnp.concatenate([dc * fc - ds * fs, dc * fs + ds * fc], 0).astype(BF16)


def modes_over_rows(first, step, out_ref):
    rows, width = out_ref.shape
    for lane in range(0, width, LANES):
        cols = slice(lane, lane + LANES)
        term, ratio = first[:, :, cols], step[:, :, cols]
        for a in range(rows // SUB):
            out_ref[a * SUB : (a + 1) * SUB, cols] = jnp.sum(term, axis=0)
            if a + 1 < rows // SUB:
                term = term * ratio


def end_state(signal_ref, step, last):
    rows, width = signal_ref.shape
    parts = []
    for lane in range(0, width, LANES):
        cols = slice(lane, lane + LANES)
        ratio = step[:, :, cols]
        total = jnp.broadcast_to(signal_ref[0:SUB, cols][None], ratio.shape)
        for a in range(1, rows // SUB):
            total = total * ratio + signal_ref[a * SUB : (a + 1) * SUB, cols][None]
        parts.append(jnp.sum(total * last[:, :, cols], axis=1))
    return jnp.concatenate(parts, 1)


def plane_size(n):
    size = 1
    while n % (2 * size) == 0 and 4 * size * size <= n:
        size *= 2
    return size


def hand_out(a_ref, b_ref, pa_ref, pb_ref, sem):
    copies = [
        pltpu.make_async_copy(a_ref, pa_ref, sem.at[0]),
        pltpu.make_async_copy(b_ref, pb_ref, sem.at[1]),
    ]
    for copy in copies:
        copy.start()
    for copy in copies:
        copy.wait()


def kernel(n, *refs):
    hbm = refs[:15]
    pa_ref, pb_ref = refs[15:17]
    vm = refs[17:32]
    (product_ref, rim_ref, filt_ref, signal_ref, carry_ref, state_ref, states_ref) = refs[32:39]
    (load_sem, rim_send, rim_recv, st_send, st_recv, far_sem) = refs[39:]
    me = lax.axis_index("seq")
    rows, width = vm[0].shape
    modes = vm[9].shape[0]

    plane = plane_size(n)
    planes = n // plane
    level, place = me // plane, lax.rem(me, plane)
    barrier = pltpu.get_barrier_semaphore()

    def signal(sem, target):
        pl.semaphore_signal(sem, inc=1, device_id={"seq": target}, device_id_type=MESH)

    @pl.loop(1, plane)
    def _(i):
        signal(barrier, level * plane + lax.rem(place + i, plane))

    @pl.loop(level + 1, planes)
    def _(i):
        signal(barrier, i * plane + place)

    @pl.when(jnp.logical_and(place == 0, level > 0))
    def _():
        signal(barrier, me - 1)

    loads = [pltpu.make_async_copy(h, v, load_sem.at[i]) for i, (h, v) in enumerate(zip(hbm, vm))]
    order = (0, 1, 2, 3, 12, 4, 9, 10, 13, 14, 5, 6, 7, 8, 11)
    for i in order:
        loads[i].start()
    (tok, rms_a, gain_a, proj_a, taps, out_a) = vm[:6]
    (rms_b, gain_b, proj_b, rates_ref, resid_ref, out_b, own_f, rim_f, back_f) = vm[6:]

    for i in (0, 1, 2, 3):
        loads[i].wait()
    normed = scaled(tok[...], column(rms_a[...]), gain_a[...])
    projected = dot(normed, proj_a[...])
    queries = projected[:, :width]
    product = (projected[:, width : 2 * width] * projected[:, 2 * width :]).astype(BF16)
    product_ref[...] = product

    crossing = jnp.logical_and(place == plane - 1, level < planes - 1)
    pl.semaphore_wait(barrier, plane - 1 + level + crossing.astype(jnp.int32))

    rim_copy = pltpu.make_async_remote_copy(
        src_ref=product_ref,
        dst_ref=rim_ref,
        send_sem=rim_send,
        recv_sem=rim_recv,
        device_id={"seq": lax.rem(me + 1, n)},
        device_id_type=MESH,
    )

    @pl.when(me < n - 1)
    def _():
        rim_copy.start()

    @pl.loop(0, level)
    def _(i):
        signal(far_sem, i * plane + place)

    loads[12].wait()
    loads[4].wait()
    spectrum = dot(own_f[...], product)
    taps_spec = dot(own_f[...], taps[...])

    loads[9].wait()
    loads[10].wait()
    rates = rates_ref[...]
    length = float(n * rows)
    weights = resid_ref[...] * jnp.sqrt(
        one_minus_exp(2.0 * rates) / one_minus_exp(2.0 * rates * length)
    )
    rates3 = jnp.broadcast_to(rates[:, None, :], (modes, SUB, width))
    within = lax.broadcasted_iota(jnp.int32, (modes, SUB, width), 1).astype(F32)
    step = jnp.exp(-rates3 * float(SUB))
    lag = jnp.exp(-rates3 * within)
    last = jnp.exp(-rates3 * (SUB - 1.0 - within))
    read = jnp.exp(-rates3 * (within + 1.0))
    block = jnp.exp(-rates * float(rows))
    modes_over_rows(weights[:, None, :] * lag, step, filt_ref)
    high, low = split(filt_ref[...])
    long_spec = dot(own_f[...], high) + dot(own_f[...], low)
    for i in (13, 14, 5, 6, 7, 8, 11):
        loads[i].wait()
    scale_b = column(rms_b[...])

    @pl.when(me > 0)
    def _():
        rim_copy.wait_recv()
        carry_ref[...] = dot(rim_f[...], rim_ref[...])

    @pl.when(me == 0)
    def _():
        carry_ref[...] = jnp.zeros_like(carry_ref)

    short_out = dot(back_f[...], spectral_product(spectrum + carry_ref[...], taps_spec))
    gated_a = (queries * short_out).astype(BF16)
    partial_a = dot(gated_a, out_a[...]).astype(BF16)
    pa_ref[...] = partial_a
    hidden = (tok[...].astype(F32) + partial_a.astype(F32)).astype(BF16)
    normed_b = scaled(hidden, scale_b, gain_b[...])
    pair_b = dot(normed_b, proj_b[:, width:])
    signal = (pair_b[:, :width] * pair_b[:, width:]).astype(BF16)
    signal_ref[...] = signal.astype(F32)
    state_ref[...] = end_state(signal_ref, step, last).astype(BF16)

    def state_copy(source, target):
        return pltpu.make_async_remote_copy(
            src_ref=state_ref,
            dst_ref=states_ref.at[source],
            send_sem=st_send.at[target],
            recv_sem=st_recv.at[source],
            device_id={"seq": target},
            device_id_type=MESH,
        )

    @pl.loop(me + 1, (level + 1) * plane)
    def _(target):
        state_copy(me, target).start()

    @pl.when(level < planes - 1)
    def _():
        pl.semaphore_wait(far_sem, planes - 1 - level)

    @pl.loop(0, plane)
    def _(i):
        @pl.loop(0, planes - 1 - level)
        def _(k):
            state_copy(me, (planes - 1 - k) * plane + i).start()


    queries_b = dot(normed_b, proj_b[:, :width])
    local = dot(back_f[...], spectral_product(dot(own_f[...], signal), long_spec))

    def gather(source, total):
        state_copy(source, lax.rem(me + 1, n)).wait_recv()
        return total * block + states_ref[source].astype(F32)

    total = lax.fori_loop(0, me, gather, jnp.zeros((modes, width), F32))
    modes_over_rows((total * weights)[:, None, :] * read, step, filt_ref)
    long_out = (local + filt_ref[...]).astype(BF16)
    gated_b = (queries_b * long_out.astype(F32)).astype(BF16)
    pb_ref[...] = dot(gated_b, out_b[...]).astype(BF16)

    @pl.when(me < n - 1)
    def _():
        rim_copy.wait_send()

    @pl.loop(0, n - 1 - me)
    def _(i):
        state_copy(me, n - 1 - i).wait_send()


def solution(mesh):
    n = mesh.shape["seq"]

    def on_device(*args):
        rows, width = args[0].shape
        modes = args[9].shape[0]
        args = [a[None] if a.ndim == 1 else a for a in args] + dft_tables(rows)
        block = jax.ShapeDtypeStruct((rows, width), BF16)
        fast = pltpu.VMEM((rows, width), BF16)
        inside = pl.BlockSpec(memory_space=pltpu.VMEM)
        anywhere = pl.BlockSpec(memory_space=pl.ANY)
        results = pl.pallas_call(
            functools.partial(kernel, n),
            out_shape=(fast, fast),
            in_specs=[anywhere] * len(args),
            out_specs=(inside, inside),
            scratch_shapes=[pltpu.VMEM(a.shape, a.dtype) for a in args]
            + [
                pltpu.VMEM((rows, width), BF16),
                pltpu.VMEM((rows, width), BF16),
                pltpu.VMEM((rows, width), F32),
                pltpu.VMEM((rows, width), F32),
                pltpu.VMEM((2 * rows, width), F32),
                pltpu.VMEM((modes, width), BF16),
                pltpu.VMEM((n, modes, width), BF16),
                pltpu.SemaphoreType.DMA((len(args),)),
                pltpu.SemaphoreType.DMA,
                pltpu.SemaphoreType.DMA,
                pltpu.SemaphoreType.DMA((n,)),
                pltpu.SemaphoreType.DMA((n,)),
                pltpu.SemaphoreType.REGULAR,
            ],
            compiler_params=pltpu.CompilerParams(collective_id=0, has_side_effects=True),
        )(*args)
        return pl.pallas_call(
            hand_out,
            out_shape=(block, block),
            in_specs=[inside] * 2,
            out_specs=(anywhere, anywhere),
            scratch_shapes=[pltpu.SemaphoreType.DMA((2,))],
        )(*[pltpu.with_memory_space_constraint(r, pltpu.VMEM) for r in results])

    shard = P(("groups", "seq"))
    wide = P(("groups", "seq"), None)
    placed = (wide, shard, P(), P(), P(), P(), shard, P(), P(), P(), P(), P())
    return jax.shard_map(
        on_device, mesh=mesh, in_specs=placed, out_specs=(wide, wide), check_vma=False
    )
```

profile of v0, /device:TPU:19, one launch (start us, length us, event | category | flops | bytes accessed | tf_op | source)
XLA Modules:
  0.0 11.0 jit_solution(375361841407586796)
XLA Ops:
  0.6 9.7 %shard_map.158 = (bf16[128,256]{1,0:T(8,128)(2,1)S(1)}, bf16[128,256]{1,0:T(8,128)(2,1)S(1)}) custom-call(bf16[128,256]{1,0:T(8,128)(2,1)} %refs_0_.1, f32[1,128]{1,0:T(1,128)} %bitcast.6, f32[1,256]{1,0:T(1,128)} %bitcast.4, bf16[256,768]{1,0:T(8,128)(2,1)} %refs_3_.1, bf16[128,256]{1,0:T(8,128)(2,1)} %refs_4_.1, bf16[256,256]{1,0:T(8,128)(2,1)} %refs_5_.1, ...), custom_call_target="tpu_custom_call" | custom-call | tf_op jit(solution)/shard_map/pallas_call | solution.py:274
  10.3 0.7 %shard_map.159 = (bf16[128,256]{1,0:T(8,128)(2,1)}, bf16[128,256]{1,0:T(8,128)(2,1)}) custom-call(bf16[128,256]{1,0:T(8,128)(2,1)S(1)} %get-tuple-element.4.a_ref, bf16[128,256]{1,0:T(8,128)(2,1)S(1)} %get-tuple-element.5.b_ref), custom_call_target="tpu_custom_call" | custom-call | tf_op jit(solution)/shard_map/pallas_call | solution.py:297
where the time goes:
time: 11.1 us; the launch traced here: 11 us
  Pallas kernels  10.3 us (93%)
  between operations  0.64 us (6%)
    pallas_call x1, Pallas kernels, on_device(): pl.pallas_call(functools.partial(kernel, n), out_shape=(fast, fast), in_s...  9.66 us
    pallas_call x1, Pallas kernels, on_device(): pl.pallas_call(hand_out, out_shape=(block, block), in_specs=[inside] * 2,...  0.67 us

commit v1 on v0

--- a/solution.py
+++ b/solution.py
@@ -13,6 +13,7 @@
 BF16 = jnp.bfloat16
 SUB = 8
 LANES = 128
+QUAD = 4
 
 
 def dft_tables(rows):
@@ -84,13 +85,6 @@
     return jnp.concatenate(parts, 1)
 
 
-def plane_size(n):
-    size = 1
-    while n % (2 * size) == 0 and 4 * size * size <= n:
-        size *= 2
-    return size
-
-
 def hand_out(a_ref, b_ref, pa_ref, pb_ref, sem):
     copies = [
         pltpu.make_async_copy(a_ref, pa_ref, sem.at[0]),
@@ -106,31 +100,42 @@
     hbm = refs[:15]
     pa_ref, pb_ref = refs[15:17]
     vm = refs[17:32]
-    (product_ref, rim_ref, filt_ref, signal_ref, carry_ref, state_ref, states_ref) = refs[32:39]
-    (load_sem, rim_send, rim_recv, st_send, st_recv, far_sem) = refs[39:]
+    (product_ref, rim_ref, filt_ref, signal_ref) = refs[32:36]
+    (own_ref, mate_ref, pair_ref, front_ref, rear_ref, extra_ref) = refs[36:42]
+    (load_sem, rim_send, rim_recv, mate_send, mate_recv) = refs[42:47]
+    (near_send, far_send, front_recv, rear_recv, far_sem) = refs[47:]
     me = lax.axis_index("seq")
     rows, width = vm[0].shape
     modes = vm[9].shape[0]
 
-    plane = plane_size(n)
-    planes = n // plane
-    level, place = me // plane, lax.rem(me, plane)
+    levels = n // QUAD
+    level, place = me // QUAD, lax.rem(me, QUAD)
+    base = level * QUAD
+    mate = me + 1 - 2 * lax.rem(me, 2)
+    speaker = (level == 0).astype(jnp.int32)
+    front = place == speaker
+    rear = place == 2
+    speaks = jnp.logical_or(front, rear)
+    greets = jnp.logical_or(place == 0, place == 2)
+    seat = jnp.where(rear, 2, 0)
     barrier = pltpu.get_barrier_semaphore()
 
     def signal(sem, target):
         pl.semaphore_signal(sem, inc=1, device_id={"seq": target}, device_id_type=MESH)
 
-    @pl.loop(1, plane)
+    @pl.when(jnp.logical_and(place == 0, level > 0))
+    def _():
+        signal(barrier, me - 1)
+
+    @pl.loop(1, QUAD)
     def _(i):
-        signal(barrier, level * plane + lax.rem(place + i, plane))
-
-    @pl.loop(level + 1, planes)
-    def _(i):
-        signal(barrier, i * plane + place)
-
-    @pl.when(jnp.logical_and(place == 0, level > 0))
-    def _():
-        signal(barrier, me - 1)
+        signal(barrier, base + lax.rem(place + QUAD - i, QUAD))
+
+    @pl.when(speaks)
+    def _():
+        @pl.loop(level + 1, levels)
+        def _(i):
+            signal(barrier, i * QUAD + seat)
 
     loads = [pltpu.make_async_copy(h, v, load_sem.at[i]) for i, (h, v) in enumerate(zip(hbm, vm))]
     order = (0, 1, 2, 3, 12, 4, 9, 10, 13, 14, 5, 6, 7, 8, 11)
@@ -138,6 +143,23 @@
         loads[i].start()
     (tok, rms_a, gain_a, proj_a, taps, out_a) = vm[:6]
     (rms_b, gain_b, proj_b, rates_ref, resid_ref, out_b, own_f, rim_f, back_f) = vm[6:]
+
+    @pl.when(me == 0)
+    def _():
+        rim_ref[...] = jnp.zeros_like(rim_ref)
+
+    crossing = jnp.logical_and(place == QUAD - 1, level < levels - 1)
+    arrivals = QUAD - 1 + jnp.where(greets, level, 0) + crossing.astype(jnp.int32)
+
+    def greet():
+        @pl.loop(0, level)
+        def _(i):
+            signal(far_sem, i * QUAD + jnp.where(rear, 2, (i == 0).astype(jnp.int32)))
+
+    @pl.when(rear)
+    def _():
+        pl.semaphore_wait(barrier, arrivals)
+        greet()
 
     for i in (0, 1, 2, 3):
         loads[i].wait()
@@ -147,8 +169,9 @@
     product = (projected[:, width : 2 * width] * projected[:, 2 * width :]).astype(BF16)
     product_ref[...] = product
 
-    crossing = jnp.logical_and(place == plane - 1, level < planes - 1)
-    pl.semaphore_wait(barrier, plane - 1 + level + crossing.astype(jnp.int32))
+    @pl.when(jnp.logical_not(rear))
+    def _():
+        pl.semaphore_wait(barrier, arrivals)
 
     rim_copy = pltpu.make_async_remote_copy(
         src_ref=product_ref,
@@ -163,9 +186,9 @@
     def _():
         rim_copy.start()
 
-    @pl.loop(0, level)
-    def _(i):
-        signal(far_sem, i * plane + place)
+    @pl.when(place == 0)
+    def _():
+        greet()
 
     loads[12].wait()
     loads[4].wait()
@@ -186,6 +209,9 @@
     last = jnp.exp(-rates3 * (SUB - 1.0 - within))
     read = jnp.exp(-rates3 * (within + 1.0))
     block = jnp.exp(-rates * float(rows))
+    two_blocks = jnp.exp(-rates * float(2 * rows))
+    four_blocks = jnp.exp(-rates * float(4 * rows))
+    seated = jnp.exp(-rates * (place * rows).astype(F32))
     modes_over_rows(weights[:, None, :] * lag, step, filt_ref)
     high, low = split(filt_ref[...])
     long_spec = dot(own_f[...], high) + dot(own_f[...], low)
@@ -196,56 +222,100 @@
     @pl.when(me > 0)
     def _():
         rim_copy.wait_recv()
-        carry_ref[...] = dot(rim_f[...], rim_ref[...])
-
-    @pl.when(me == 0)
-    def _():
-        carry_ref[...] = jnp.zeros_like(carry_ref)
-
-    short_out = dot(back_f[...], spectral_product(spectrum + carry_ref[...], taps_spec))
+
+    carry = dot(rim_f[...], rim_ref[...])
+    short_out = dot(back_f[...], spectral_product(spectrum + carry, taps_spec))
     gated_a = (queries * short_out).astype(BF16)
     partial_a = dot(gated_a, out_a[...]).astype(BF16)
     pa_ref[...] = partial_a
     hidden = (tok[...].astype(F32) + partial_a.astype(F32)).astype(BF16)
     normed_b = scaled(hidden, scale_b, gain_b[...])
     pair_b = dot(normed_b, proj_b[:, width:])
-    signal = (pair_b[:, :width] * pair_b[:, width:]).astype(BF16)
-    signal_ref[...] = signal.astype(F32)
-    state_ref[...] = end_state(signal_ref, step, last).astype(BF16)
-
-    def state_copy(source, target):
+    signal_b = (pair_b[:, :width] * pair_b[:, width:]).astype(BF16)
+    signal_ref[...] = signal_b.astype(F32)
+    state = end_state(signal_ref, step, last)
+    own_ref[...] = state
+
+    mate_copy = pltpu.make_async_remote_copy(
+        src_ref=own_ref,
+        dst_ref=mate_ref,
+        send_sem=mate_send,
+        recv_sem=mate_recv,
+        device_id={"seq": mate},
+        device_id_type=MESH,
+    )
+    mate_copy.start()
+
+    def front_copy(source, target, sem):
         return pltpu.make_async_remote_copy(
-            src_ref=state_ref,
-            dst_ref=states_ref.at[source],
-            send_sem=st_send.at[target],
-            recv_sem=st_recv.at[source],
+            src_ref=pair_ref,
+            dst_ref=front_ref.at[source],
+            send_sem=sem,
+            recv_sem=front_recv.at[source],
             device_id={"seq": target},
             device_id_type=MESH,
         )
 
-    @pl.loop(me + 1, (level + 1) * plane)
-    def _(target):
-        state_copy(me, target).start()
-
-    @pl.when(level < planes - 1)
-    def _():
-        pl.semaphore_wait(far_sem, planes - 1 - level)
-
-    @pl.loop(0, plane)
-    def _(i):
-        @pl.loop(0, planes - 1 - level)
-        def _(k):
-            state_copy(me, (planes - 1 - k) * plane + i).start()
-
+    def rear_copy(source, target, sem):
+        return pltpu.make_async_remote_copy(
+            src_ref=pair_ref,
+            dst_ref=rear_ref.at[source],
+            send_sem=sem,
+            recv_sem=rear_recv.at[source],
+            device_id={"seq": target},
+            device_id_type=MESH,
+        )
+
+    mate_copy.wait_recv()
+    early = lax.rem(place, 2) == 0
+    pair_ref[...] = (
+        jnp.where(early, state, mate_ref[...]) * block + jnp.where(early, mate_ref[...], state)
+    ).astype(BF16)
+
+    @pl.when(front)
+    def _():
+        for i in (1, 0):
+            front_copy(level, base + 2 + i, near_send.at[i]).start()
+
+    @pl.when(jnp.logical_and(speaks, level < levels - 1))
+    def _():
+        pl.semaphore_wait(far_sem, levels - 1 - level)
+
+    def spread(copy, seats):
+        for seat_there in seats:
+            @pl.loop(level + 1, levels)
+            def _(there):
+                target = there * QUAD + seat_there
+                copy(level, target, far_send.at[target]).start()
+
+    @pl.when(front)
+    def _():
+        spread(front_copy, (1, 3, 0, 2))
+
+    @pl.when(rear)
+    def _():
+        spread(rear_copy, (1, 0, 3, 2))
 
     queries_b = dot(normed_b, proj_b[:, :width])
-    local = dot(back_f[...], spectral_product(dot(own_f[...], signal), long_spec))
+    local = dot(back_f[...], spectral_product(dot(own_f[...], signal_b), long_spec))
+
+    extra_ref[...] = jnp.where(place == 0, jnp.zeros_like(state), mate_ref[...])
 
     def gather(source, total):
-        state_copy(source, lax.rem(me + 1, n)).wait_recv()
-        return total * block + states_ref[source].astype(F32)
-
-    total = lax.fori_loop(0, me, gather, jnp.zeros((modes, width), F32))
+        front_copy(source, mate, far_send.at[0]).wait_recv()
+        pairs = front_ref[source].astype(F32) * two_blocks
+        rear_copy(source, mate, far_send.at[0]).wait_recv()
+        return total * four_blocks + (pairs + rear_ref[source].astype(F32))
+
+    total = lax.fori_loop(0, level, gather, jnp.zeros((modes, width), F32))
+
+    @pl.when(place >= 2)
+    def _():
+        front_copy(level, mate, far_send.at[0]).wait_recv()
+        pairs = front_ref[level].astype(F32)
+        extra_ref[...] = jnp.where(place == 2, pairs, pairs * block + extra_ref[...])
+
+    total = total * seated + extra_ref[...]
     modes_over_rows((total * weights)[:, None, :] * read, step, filt_ref)
     long_out = (local + filt_ref[...]).astype(BF16)
     gated_b = (queries_b * long_out.astype(F32)).astype(BF16)
@@ -255,13 +325,23 @@
     def _():
         rim_copy.wait_send()
 
-    @pl.loop(0, n - 1 - me)
-    def _(i):
-        state_copy(me, n - 1 - i).wait_send()
+    mate_copy.wait_send()
+
+    @pl.when(front)
+    def _():
+        for i in (0, 1):
+            front_copy(level, base + 2 + i, near_send.at[i]).wait_send()
+
+    @pl.when(speaks)
+    def _():
+        @pl.loop(base + QUAD, n)
+        def _(target):
+            front_copy(level, target, far_send.at[target]).wait_send()
 
 
 def solution(mesh):
     n = mesh.shape["seq"]
+    assert n % QUAD == 0
 
     def on_device(*args):
         rows, width = args[0].shape
@@ -282,14 +362,21 @@
                 pltpu.VMEM((rows, width), BF16),
                 pltpu.VMEM((rows, width), F32),
                 pltpu.VMEM((rows, width), F32),
-                pltpu.VMEM((2 * rows, width), F32),
+                pltpu.VMEM((modes, width), F32),
+                pltpu.VMEM((modes, width), F32),
                 pltpu.VMEM((modes, width), BF16),
-                pltpu.VMEM((n, modes, width), BF16),
+                pltpu.VMEM((n // QUAD, modes, width), BF16),
+                pltpu.VMEM((n // QUAD, modes, width), BF16),
+                pltpu.VMEM((modes, width), F32),
                 pltpu.SemaphoreType.DMA((len(args),)),
                 pltpu.SemaphoreType.DMA,
                 pltpu.SemaphoreType.DMA,
+                pltpu.SemaphoreType.DMA,
+                pltpu.SemaphoreType.DMA,
+                pltpu.SemaphoreType.DMA((2,)),
                 pltpu.SemaphoreType.DMA((n,)),
-                pltpu.SemaphoreType.DMA((n,)),
+                pltpu.SemaphoreType.DMA((n // QUAD,)),
+                pltpu.SemaphoreType.DMA((n // QUAD,)),
                 pltpu.SemaphoreType.REGULAR,
             ],
             compiler_params=pltpu.CompilerParams(collective_id=0, has_side_effects=True),

time: 11.1 us -> 10.7 us (0.964)
  the two profiles are of different devices: /device:TPU:19 before, /device:TPU:28 now
where the time goes in v1:
time: 10.7 us; the launch traced here: 10.5 us
  Pallas kernels  9.9 us (93%)
  between operations  0.64 us (6%)
    pallas_call x1, Pallas kernels, on_device(): pl.pallas_call(functools.partial(kernel, n), out_shape=(fast, fast), in_s...  9.23 us
    pallas_call x1, Pallas kernels, on_device(): pl.pallas_call(hand_out, out_shape=(block, block), in_specs=[inside] * 2,...  0.67 us

profile of v1, /device:TPU:28, one launch (start us, length us, event | category | flops | bytes accessed | tf_op | source)
XLA Modules:
  0.0 10.5 jit_solution(5023622900545555331)
XLA Ops:
  0.6 9.2 %shard_map.158 = (bf16[128,256]{1,0:T(8,128)(2,1)S(1)}, bf16[128,256]{1,0:T(8,128)(2,1)S(1)}) custom-call(bf16[128,256]{1,0:T(8,128)(2,1)} %refs_0_.1, f32[1,128]{1,0:T(1,128)} %bitcast.6, f32[1,256]{1,0:T(1,128)} %bitcast.4, bf16[256,768]{1,0:T(8,128)(2,1)} %refs_3_.1, bf16[128,256]{1,0:T(8,128)(2,1)} %refs_4_.1, bf16[256,256]{1,0:T(8,128)(2,1)} %refs_5_.1, ...), custom_call_target="tpu_custom_call" | custom-call | tf_op jit(solution)/shard_map/pallas_call | solution.py:354
  9.9 0.7 %shard_map.159 = (bf16[128,256]{1,0:T(8,128)(2,1)}, bf16[128,256]{1,0:T(8,128)(2,1)}) custom-call(bf16[128,256]{1,0:T(8,128)(2,1)S(1)} %get-tuple-element.4.a_ref, bf16[128,256]{1,0:T(8,128)(2,1)S(1)} %get-tuple-element.5.b_ref), custom_call_target="tpu_custom_call" | custom-call | tf_op jit(solution)/shard_map/pallas_call | solution.py:384

commit v2 on v1

--- a/solution.py
+++ b/solution.py
@@ -72,17 +72,41 @@
                 term = term * ratio
 
 
-def end_state(signal_ref, step, last):
-    rows, width = signal_ref.shape
-    parts = []
+def sublane_sums(parts):
+    row = lax.broadcasted_iota(jnp.int32, parts[0].shape, 0)
+    high = row >= 4
+    parts = [
+        jnp.where(high, b, a) + pltpu.roll(jnp.where(high, a, b), 4, 0)
+        for a, b in zip(parts[:4], parts[4:])
+    ]
+    for shift in (2, 1):
+        odd = lax.rem(row // shift, 2) == 1
+        count = len(parts) // 2
+        parts = [
+            jnp.where(odd, b + pltpu.roll(b, shift, 0), a + pltpu.roll(a, SUB - shift, 0))
+            for a, b in zip(parts[:count], parts[count:])
+        ]
+    return parts[0]
+
+
+def end_state(signal, step, last):
+    rows, width = signal.shape
+    modes = step.shape[0]
+    columns = []
     for lane in range(0, width, LANES):
         cols = slice(lane, lane + LANES)
-        ratio = step[:, :, cols]
-        total = jnp.broadcast_to(signal_ref[0:SUB, cols][None], ratio.shape)
-        for a in range(1, rows // SUB):
-            total = total * ratio + signal_ref[a * SUB : (a + 1) * SUB, cols][None]
-        parts.append(jnp.sum(total * last[:, :, cols], axis=1))
-    return jnp.concatenate(parts, 1)
+        tiles = [signal[r : r + SUB, cols] for r in range(0, rows, SUB)]
+        groups = []
+        for first in range(0, modes, SUB):
+            parts = []
+            for m in range(first, first + SUB):
+                ratio, total = step[m, :, cols], tiles[0]
+                for tile in tiles[1:]:
+                    total = total * ratio + tile
+                parts.append(total * last[m, :, cols])
+            groups.append(sublane_sums(parts))
+        columns.append(jnp.concatenate(groups, 0))
+    return jnp.concatenate(columns, 1)
 
 
 def hand_out(a_ref, b_ref, pa_ref, pb_ref, sem):
@@ -100,7 +124,7 @@
     hbm = refs[:15]
     pa_ref, pb_ref = refs[15:17]
     vm = refs[17:32]
-    (product_ref, rim_ref, filt_ref, signal_ref) = refs[32:36]
+    (tail_ref, rim_ref, filt_ref, signal_ref) = refs[32:36]
     (own_ref, mate_ref, pair_ref, front_ref, rear_ref, extra_ref) = refs[36:42]
     (load_sem, rim_send, rim_recv, mate_send, mate_recv) = refs[42:47]
     (near_send, far_send, front_recv, rear_recv, far_sem) = refs[47:]
@@ -116,8 +140,6 @@
     front = place == speaker
     rear = place == 2
     speaks = jnp.logical_or(front, rear)
-    greets = jnp.logical_or(place == 0, place == 2)
-    seat = jnp.where(rear, 2, 0)
     barrier = pltpu.get_barrier_semaphore()
 
     def signal(sem, target):
@@ -135,10 +157,10 @@
     def _():
         @pl.loop(level + 1, levels)
         def _(i):
-            signal(barrier, i * QUAD + seat)
+            signal(barrier, i * QUAD + 2)
 
     loads = [pltpu.make_async_copy(h, v, load_sem.at[i]) for i, (h, v) in enumerate(zip(hbm, vm))]
-    order = (0, 1, 2, 3, 12, 4, 9, 10, 13, 14, 5, 6, 7, 8, 11)
+    order = (0, 1, 2, 3, 12, 4, 13, 14, 9, 10, 5, 6, 7, 8, 11)
     for i in order:
         loads[i].start()
     (tok, rms_a, gain_a, proj_a, taps, out_a) = vm[:6]
@@ -149,17 +171,15 @@
         rim_ref[...] = jnp.zeros_like(rim_ref)
 
     crossing = jnp.logical_and(place == QUAD - 1, level < levels - 1)
-    arrivals = QUAD - 1 + jnp.where(greets, level, 0) + crossing.astype(jnp.int32)
-
-    def greet():
+
+    @pl.when(rear)
+    def _():
+        pl.semaphore_wait(barrier, QUAD - 1 + 2 * level)
+
         @pl.loop(0, level)
         def _(i):
-            signal(far_sem, i * QUAD + jnp.where(rear, 2, (i == 0).astype(jnp.int32)))
-
-    @pl.when(rear)
-    def _():
-        pl.semaphore_wait(barrier, arrivals)
-        greet()
+            signal(far_sem, i * QUAD + (i == 0).astype(jnp.int32))
+            signal(far_sem, i * QUAD + 2)
 
     for i in (0, 1, 2, 3):
         loads[i].wait()
@@ -167,14 +187,19 @@
     projected = dot(normed, proj_a[...])
     queries = projected[:, :width]
     product = (projected[:, width : 2 * width] * projected[:, 2 * width :]).astype(BF16)
-    product_ref[...] = product
+    for i in (12, 4, 13, 14):
+        loads[i].wait()
+    taps_spec = dot(own_f[...], taps[...])
+    tail_ref[...] = dot(
+        back_f[...], spectral_product(dot(rim_f[...], product), taps_spec)
+    ).astype(BF16)
 
     @pl.when(jnp.logical_not(rear))
     def _():
-        pl.semaphore_wait(barrier, arrivals)
+        pl.semaphore_wait(barrier, QUAD - 1 + crossing.astype(jnp.int32))
 
     rim_copy = pltpu.make_async_remote_copy(
-        src_ref=product_ref,
+        src_ref=tail_ref,
         dst_ref=rim_ref,
         send_sem=rim_send,
         recv_sem=rim_recv,
@@ -186,51 +211,31 @@
     def _():
         rim_copy.start()
 
-    @pl.when(place == 0)
-    def _():
-        greet()
-
-    loads[12].wait()
-    loads[4].wait()
-    spectrum = dot(own_f[...], product)
-    taps_spec = dot(own_f[...], taps[...])
+    short_own = dot(back_f[...], spectral_product(dot(own_f[...], product), taps_spec))
 
     loads[9].wait()
     loads[10].wait()
     rates = rates_ref[...]
     length = float(n * rows)
-    weights = resid_ref[...] * jnp.sqrt(
-        one_minus_exp(2.0 * rates) / one_minus_exp(2.0 * rates * length)
-    )
     rates3 = jnp.broadcast_to(rates[:, None, :], (modes, SUB, width))
     within = lax.broadcasted_iota(jnp.int32, (modes, SUB, width), 1).astype(F32)
     step = jnp.exp(-rates3 * float(SUB))
-    lag = jnp.exp(-rates3 * within)
     last = jnp.exp(-rates3 * (SUB - 1.0 - within))
-    read = jnp.exp(-rates3 * (within + 1.0))
     block = jnp.exp(-rates * float(rows))
-    two_blocks = jnp.exp(-rates * float(2 * rows))
-    four_blocks = jnp.exp(-rates * float(4 * rows))
-    seated = jnp.exp(-rates * (place * rows).astype(F32))
-    modes_over_rows(weights[:, None, :] * lag, step, filt_ref)
-    high, low = split(filt_ref[...])
-    long_spec = dot(own_f[...], high) + dot(own_f[...], low)
-    for i in (13, 14, 5, 6, 7, 8, 11):
+    for i in (5, 6, 7, 8, 11):
         loads[i].wait()
     scale_b = column(rms_b[...])
+    base_b = dot(scaled(tok[...], scale_b, gain_b[...]), proj_b[...])
+    high, low = split(out_a[...].astype(F32) * gain_b[...])
+    through = (dot(high, proj_b[...]) + dot(low, proj_b[...])).astype(BF16)
 
     @pl.when(me > 0)
     def _():
         rim_copy.wait_recv()
 
-    carry = dot(rim_f[...], rim_ref[...])
-    short_out = dot(back_f[...], spectral_product(spectrum + carry, taps_spec))
+    short_out = short_own + rim_ref[...].astype(F32)
     gated_a = (queries * short_out).astype(BF16)
-    partial_a = dot(gated_a, out_a[...]).astype(BF16)
-    pa_ref[...] = partial_a
-    hidden = (tok[...].astype(F32) + partial_a.astype(F32)).astype(BF16)
-    normed_b = scaled(hidden, scale_b, gain_b[...])
-    pair_b = dot(normed_b, proj_b[:, width:])
+    pair_b = base_b[:, width:] + scale_b * dot(gated_a, through[:, width:])
     signal_b = (pair_b[:, :width] * pair_b[:, width:]).astype(BF16)
     signal_ref[...] = signal_b.astype(F32)
     state = end_state(signal_ref, step, last)
@@ -282,21 +287,34 @@
         pl.semaphore_wait(far_sem, levels - 1 - level)
 
     def spread(copy, seats):
-        for seat_there in seats:
-            @pl.loop(level + 1, levels)
-            def _(there):
+        for seat_there, outward in seats:
+            @pl.loop(0, levels - 1 - level)
+            def _(i):
+                there = level + 1 + i if outward else levels - 1 - i
                 target = there * QUAD + seat_there
                 copy(level, target, far_send.at[target]).start()
 
     @pl.when(front)
     def _():
-        spread(front_copy, (1, 3, 0, 2))
+        spread(front_copy, ((1, False), (0, False), (3, False), (2, False)))
 
     @pl.when(rear)
     def _():
-        spread(rear_copy, (1, 0, 3, 2))
-
-    queries_b = dot(normed_b, proj_b[:, :width])
+        spread(rear_copy, ((1, False), (0, True), (3, False), (2, False)))
+
+    pa_ref[...] = dot(gated_a, out_a[...]).astype(BF16)
+    queries_b = base_b[:, :width] + scale_b * dot(gated_a, through[:, :width])
+    length = float(n * rows)
+    weights = resid_ref[...] * jnp.sqrt(
+        one_minus_exp(2.0 * rates) / one_minus_exp(2.0 * rates * length)
+    )
+    modes_over_rows(weights[:, None, :] * jnp.exp(-rates3 * within), step, filt_ref)
+    high, low = split(filt_ref[...])
+    long_spec = dot(own_f[...], high) + dot(own_f[...], low)
+    read = jnp.exp(-rates3 * (within + 1.0))
+    two_blocks = jnp.exp(-rates * float(2 * rows))
+    four_blocks = jnp.exp(-rates * float(4 * rows))
+    seated = jnp.exp(-rates * (place * rows).astype(F32))
     local = dot(back_f[...], spectral_product(dot(own_f[...], signal_b), long_spec))
 
     extra_ref[...] = jnp.where(place == 0, jnp.zeros_like(state), mate_ref[...])

time: 10.7 us -> 10.3 us (0.963)
  Pallas kernels: 9.9 us -> 9.52 us
    pallas_call x1, Pallas kernels: 9.23 us -> 8.85 us  [on_device(): pl.pallas_call(functools.partial(kernel, n), out_shape=(fast, fast), in_s...]
where the time goes in v2:
time: 10.3 us; the launch traced here: 10.2 us
  Pallas kernels  9.52 us (92%)
  between operations  0.64 us (6%)
    pallas_call x1, Pallas kernels, on_device(): pl.pallas_call(functools.partial(kernel, n), out_shape=(fast, fast), in_s...  8.85 us
    pallas_call x1, Pallas kernels, on_device(): pl.pallas_call(hand_out, out_shape=(block, block), in_specs=[inside] * 2,...  0.67 us

profile of v2, /device:TPU:28, one launch (start us, length us, event | category | flops | bytes accessed | tf_op | source)
XLA Modules:
  0.0 10.2 jit_solution(2687231244330230184)
XLA Ops:
  0.6 8.8 %shard_map.158 = (bf16[128,256]{1,0:T(8,128)(2,1)S(1)}, bf16[128,256]{1,0:T(8,128)(2,1)S(1)}) custom-call(bf16[128,256]{1,0:T(8,128)(2,1)} %refs_0_.1, f32[1,128]{1,0:T(1,128)} %bitcast.6, f32[1,256]{1,0:T(1,128)} %bitcast.4, bf16[256,768]{1,0:T(8,128)(2,1)} %refs_3_.1, bf16[128,256]{1,0:T(8,128)(2,1)} %refs_4_.1, bf16[256,256]{1,0:T(8,128)(2,1)} %refs_5_.1, ...), custom_call_target="tpu_custom_call" | custom-call | tf_op jit(solution)/shard_map/pallas_call | solution.py:372
  9.5 0.7 %shard_map.159 = (bf16[128,256]{1,0:T(8,128)(2,1)}, bf16[128,256]{1,0:T(8,128)(2,1)}) custom-call(bf16[128,256]{1,0:T(8,128)(2,1)S(1)} %get-tuple-element.4.a_ref, bf16[128,256]{1,0:T(8,128)(2,1)S(1)} %get-tuple-element.5.b_ref), custom_call_target="tpu_custom_call" | custom-call | tf_op jit(solution)/shard_map/pallas_call | solution.py:402

commit v3 on v2

v3 whole, which is shorter than its diff:
```python
import functools

import jax
import jax.numpy as jnp
import numpy as np
from jax import lax
from jax.experimental import pallas as pl
from jax.experimental.pallas import tpu as pltpu
from jax.sharding import PartitionSpec as P

MESH = pl.DeviceIdType.MESH
F32 = jnp.float32
BF16 = jnp.bfloat16
SUB = 8
LANES = 128
QUAD = 4
PIECES = 2


def dft_tables(rows):
    freq = (np.arange(rows) + 0.5)[:, None]
    angle = freq * np.arange(rows)[None, :] * (np.pi / rows)
    cos, sin = np.cos(angle), np.sin(angle)
    sign = np.where(np.arange(rows) % 2 == 0, 1.0, -1.0)[:, None]
    own = np.concatenate([cos, sin], 0)
    behind = np.concatenate([sign * sin, -sign * cos], 0)
    back = own.T / rows
    return [jnp.asarray(t, F32).astype(BF16) for t in (own, behind, back)]


def dot(left, right):
    return jnp.dot(left, right, preferred_element_type=F32)


def split(value):
    high = value.astype(BF16)
    return high, (value - high.astype(F32)).astype(BF16)


def one_minus_exp(a):
    series = 1.0 - a / 9.0
    for k in (8.0, 7.0, 6.0, 5.0, 4.0, 3.0, 2.0):
        series = 1.0 - series * a / k
    return jnp.where(a < 0.5, a * series, 1.0 - jnp.exp(-a))


def column(row):
    rows = row.shape[1]
    eye = lax.broadcasted_iota(jnp.int32, (rows, rows), 0) == lax.broadcasted_iota(
        jnp.int32, (rows, rows), 1
    )
    return jnp.sum(jnp.where(eye, row, 0.0), axis=1, keepdims=True)


def scaled(tokens, scale, gain):
    return (tokens.astype(F32) * scale * gain).astype(BF16)


def spectral_product(data, filt):
    half = data.shape[0] // 2
    dc, ds, fc, fs = data[:half], data[half:], filt[:half], filt[half:]
    return jnp.concatenate([dc * fc - ds * fs, dc * fs + ds * fc], 0).astype(BF16)


def modes_over_rows(first, step, out_ref):
    rows, width = out_ref.shape
    for lane in range(0, width, LANES):
        cols = slice(lane, lane + LANES)
        term, ratio = first[:, :, cols], step[:, :, cols]
        for a in range(rows // SUB):
            out_ref[a * SUB : (a + 1) * SUB, cols] = jnp.sum(term, axis=0)
            if a + 1 < rows // SUB:
                term = term * ratio


def sublane_sums(parts):
    row = lax.broadcasted_iota(jnp.int32, parts[0].shape, 0)
    high = row >= 4
    parts = [
        jnp.where(high, b, a) + pltpu.roll(jnp.where(high, a, b), 4, 0)
        for a, b in zip(parts[:4], parts[4:])
    ]
    for shift in (2, 1):
        odd = lax.rem(row // shift, 2) == 1
        count = len(parts) // 2
        parts = [
            jnp.where(odd, b + pltpu.roll(b, shift, 0), a + pltpu.roll(a, SUB - shift, 0))
            for a, b in zip(parts[:count], parts[count:])
        ]
    return parts[0]


def end_totals(totals, signal, step):
    rows, width = signal.shape
    modes = step.shape[0]
    sums = {}
    for lane in range(0, width, LANES):
        cols = slice(lane, lane + LANES)
        tiles = [signal[r : r + SUB, cols] for r in range(0, rows, SUB)]
        for m in range(modes):
            total, rest = (tiles[0], tiles[1:]) if totals is None else (totals[lane, m], tiles)
            for tile in rest:
                total = total * step[m, :, cols] + tile
            sums[lane, m] = total
    return sums


def end_state(totals, last):
    modes, _, width = last.shape
    columns = []
    for lane in range(0, width, LANES):
        parts = [totals[lane, m] * last[m, :, lane : lane + LANES] for m in range(modes)]
        columns.append(
            jnp.concatenate([sublane_sums(parts[m : m + SUB]) for m in range(0, modes, SUB)], 0)
        )
    return jnp.concatenate(columns, 1)


def size(ref):
    return int(np.prod(ref.shape)) * ref.dtype.itemsize


def settle(span_ref, sem, total):
    part = span_ref.at[pl.ds(0, total // (LANES * 4))]
    pltpu.make_async_copy(part, part, sem).wait()


def hand_out(a_ref, b_ref, pa_ref, pb_ref, span_ref, sem):
    copies = [
        pltpu.make_async_copy(a_ref, pa_ref, sem),
        pltpu.make_async_copy(b_ref, pb_ref, sem),
    ]
    for copy in copies:
        copy.start()
    settle(span_ref, sem, size(a_ref) + size(b_ref))


def kernel(n, *refs):
    hbm = refs[:15]
    pa_ref, pb_ref = refs[15:17]
    vm = refs[17:32]
    (tail_ref, rim_ref, filt_ref, signal_ref, gated_ref) = refs[32:37]
    (own_ref, mate_ref, pair_ref, front_ref, rear_ref, extra_ref, span_ref) = refs[37:44]
    (load_sem, send_sem, rim_recv, mate_recv, far_recv, far_sem) = refs[44:]
    rows, width = vm[0].shape
    modes = vm[9].shape[0]

    groups = ((1, 2, 0), (3,), (12, 4, 13, 14), (15, 9, 10, 5, 6, 7, 8, 11))
    pairs_of = dict(enumerate(zip(hbm, vm)))
    keys = (slice(None), pl.ds(width, 2 * width))
    queries_only = (slice(None), pl.ds(0, width))
    pairs_of[3] = (hbm[3].at[keys], vm[3].at[keys])
    pairs_of[15] = (hbm[3].at[queries_only], vm[3].at[queries_only])
    loads = [
        [pltpu.make_async_copy(*pairs_of[i], load_sem.at[g]) for i in group]
        for g, group in enumerate(groups)
    ]

    def start(*which):
        for g in which:
            for load in loads[g]:
                load.start()

    def arrive(g):
        settle(span_ref, load_sem.at[g], sum(size(pairs_of[i][1]) for i in groups[g]))

    start(0, 1)
    me = lax.axis_index("seq")

    levels = n // QUAD
    level, place = me // QUAD, lax.rem(me, QUAD)
    base = level * QUAD
    mate = me + 1 - 2 * lax.rem(me, 2)
    speaker = (level == 0).astype(jnp.int32)
    front = place == speaker
    rear = place == 2
    speaks = jnp.logical_or(front, rear)
    barrier = pltpu.get_barrier_semaphore()

    def signal(sem, target):
        pl.semaphore_signal(sem, inc=1, device_id={"seq": target}, device_id_type=MESH)

    @pl.when(jnp.logical_and(place == 0, level > 0))
    def _():
        signal(barrier, me - 1)

    @pl.loop(1, QUAD)
    def _(i):
        signal(barrier, base + lax.rem(place + QUAD - i, QUAD))

    @pl.when(speaks)
    def _():
        @pl.loop(level + 1, levels)
        def _(i):
            signal(barrier, i * QUAD + 2)

    start(2, 3)
    (tok, rms_a, gain_a, proj_a, taps, out_a) = vm[:6]
    (rms_b, gain_b, proj_b, rates_ref, resid_ref, out_b, own_f, rim_f, back_f) = vm[6:]

    piece = rows // PIECES
    pieces = [pl.ds(p * piece, piece) for p in range(PIECES)]

    @pl.when(me == 0)
    def _():
        gated_ref[...] = jnp.zeros_like(gated_ref)
        for i, p in enumerate(pieces):
            pltpu.make_async_copy(gated_ref.at[p], rim_ref.at[p], rim_recv.at[i]).start()

    crossing = jnp.logical_and(place == QUAD - 1, level < levels - 1)

    @pl.when(rear)
    def _():
        pl.semaphore_wait(barrier, QUAD - 1 + 2 * level)

        @pl.loop(0, level)
        def _(i):
            signal(far_sem, i * QUAD + (i == 0).astype(jnp.int32))
            signal(far_sem, i * QUAD + 2)

    arrive(0)
    normed = scaled(tok[...], column(rms_a[...]), gain_a[...])
    arrive(1)
    pair_a = dot(normed, proj_a[:, width:])
    product = (pair_a[:, :width] * pair_a[:, width:]).astype(BF16)
    arrive(2)
    taps_spec = dot(own_f[...], taps[...])
    tail_ref[...] = dot(
        back_f[...], spectral_product(dot(rim_f[...], product), taps_spec)
    ).astype(BF16)

    @pl.when(jnp.logical_not(rear))
    def _():
        pl.semaphore_wait(barrier, QUAD - 1 + crossing.astype(jnp.int32))

    rim_copies = [
        pltpu.make_async_remote_copy(
            src_ref=tail_ref.at[p],
            dst_ref=rim_ref.at[p],
            send_sem=send_sem,
            recv_sem=rim_recv.at[i],
            device_id={"seq": lax.rem(me + 1, n)},
            device_id_type=MESH,
        )
        for i, p in enumerate(pieces)
    ]

    @pl.when(me < n - 1)
    def _():
        for copy in rim_copies:
            copy.start()

    arrive(3)
    queries = dot(normed, proj_a[:, :width])
    short_own = dot(back_f[...], spectral_product(dot(own_f[...], product), taps_spec))

    rates = rates_ref[...]
    length = float(n * rows)
    rates3 = jnp.broadcast_to(rates[:, None, :], (modes, SUB, width))
    within = lax.broadcasted_iota(jnp.int32, (modes, SUB, width), 1).astype(F32)
    step = jnp.exp(-rates3 * float(SUB))
    last = jnp.exp(-rates3 * (SUB - 1.0 - within))
    block = jnp.exp(-rates * float(rows))
    scale_b = column(rms_b[...])
    base_b = dot(scaled(tok[...], scale_b, gain_b[...]), proj_b[...])
    high, low = split(out_a[...].astype(F32) * gain_b[...])
    through = (dot(high, proj_b[...]) + dot(low, proj_b[...])).astype(BF16)

    totals = None
    for i, p in enumerate(pieces):
        rim_copies[i].wait_recv()
        span = slice(i * piece, (i + 1) * piece)
        gated = (queries[span] * (short_own[span] + rim_ref[p].astype(F32))).astype(BF16)
        gated_ref[p] = gated
        pair_b = base_b[span, width:] + scale_b[span] * dot(gated, through[:, width:])
        signal = (pair_b[:, :width] * pair_b[:, width:]).astype(BF16)
        signal_ref[p] = signal
        totals = end_totals(totals, signal.astype(F32), step)
    state = end_state(totals, last)
    own_ref[...] = state

    mate_copy = pltpu.make_async_remote_copy(
        src_ref=own_ref,
        dst_ref=mate_ref,
        send_sem=send_sem,
        recv_sem=mate_recv,
        device_id={"seq": mate},
        device_id_type=MESH,
    )
    mate_copy.start()

    def far_copy(slots, target, there):
        return pltpu.make_async_remote_copy(
            src_ref=pair_ref,
            dst_ref=slots.at[level],
            send_sem=send_sem,
            recv_sem=far_recv.at[(there - level <= 1).astype(jnp.int32)],
            device_id={"seq": target},
            device_id_type=MESH,
        )

    mate_copy.wait_recv()
    early = lax.rem(place, 2) == 0
    pair_ref[...] = (
        jnp.where(early, state, mate_ref[...]) * block + jnp.where(early, mate_ref[...], state)
    ).astype(BF16)

    @pl.when(front)
    def _():
        for i in (1, 0):
            far_copy(front_ref, base + 2 + i, level).start()

    @pl.when(jnp.logical_and(speaks, level < levels - 1))
    def _():
        pl.semaphore_wait(far_sem, levels - 1 - level)

    def spread(slots, seats):
        for seat_there, outward in seats:
            @pl.loop(0, levels - 1 - level)
            def _(i):
                there = level + 1 + i if outward else levels - 1 - i
                target = there * QUAD + seat_there
                far_copy(slots, target, there).start()

    @pl.when(front)
    def _():
        spread(front_ref, ((1, False), (0, False), (3, False), (2, False)))

    @pl.when(rear)
    def _():
        spread(rear_ref, ((1, False), (0, True), (3, False), (2, False)))

    pa_ref[...] = dot(gated_ref[...], out_a[...]).astype(BF16)
    queries_b = base_b[:, :width] + scale_b * dot(gated_ref[...], through[:, :width])
    length = float(n * rows)
    weights = resid_ref[...] * jnp.sqrt(
        one_minus_exp(2.0 * rates) / one_minus_exp(2.0 * rates * length)
    )
    modes_over_rows(weights[:, None, :] * jnp.exp(-rates3 * within), step, filt_ref)
    high, low = split(filt_ref[...])
    long_spec = dot(own_f[...], high) + dot(own_f[...], low)
    read = jnp.exp(-rates3 * (within + 1.0))
    two_blocks = jnp.exp(-rates * float(2 * rows))
    four_blocks = jnp.exp(-rates * float(4 * rows))
    seated = jnp.exp(-rates * (place * rows).astype(F32))
    local = dot(back_f[...], spectral_product(dot(own_f[...], signal_ref[...]), long_spec))

    extra_ref[...] = jnp.where(place == 0, jnp.zeros_like(state), mate_ref[...])

    always = size(rim_ref) + size(own_ref)
    letter = size(pair_ref)

    @pl.when(jnp.logical_and(jnp.logical_not(speaks), me < n - 1))
    def _():
        settle(span_ref, send_sem, always)

    @pl.when(me == n - 1)
    def _():
        settle(span_ref, send_sem, size(own_ref))

    for there in range(levels):
        rest = (levels - 1 - there) * QUAD

        @pl.when(jnp.logical_and(front, level == there))
        def _():
            settle(span_ref, send_sem, always + (rest + 2) * letter)

        @pl.when(jnp.logical_and(rear, level == there))
        def _():
            settle(span_ref, send_sem, always + rest * letter)

    def gather(source, total):
        pairs = front_ref[source].astype(F32) * two_blocks
        return total * four_blocks + (pairs + rear_ref[source].astype(F32))

    older = jnp.maximum(level - 1, 0)
    for there in range(2, levels):

        @pl.when(level == there)
        def _():
            settle(span_ref, far_recv.at[0], 2 * (there - 1) * letter)

    total = lax.fori_loop(0, older, gather, jnp.zeros((modes, width), F32))
    back = place >= 2

    @pl.when(jnp.logical_and(level > 0, jnp.logical_not(back)))
    def _():
        settle(span_ref, far_recv.at[1], 2 * letter)

    @pl.when(jnp.logical_and(level > 0, back))
    def _():
        settle(span_ref, far_recv.at[1], 3 * letter)

    @pl.when(jnp.logical_and(level == 0, back))
    def _():
        settle(span_ref, far_recv.at[1], letter)

    total = lax.fori_loop(older, level, gather, total)

    @pl.when(place >= 2)
    def _():
        pairs = front_ref[level].astype(F32)
        extra_ref[...] = jnp.where(place == 2, pairs, pairs * block + extra_ref[...])

    total = total * seated + extra_ref[...]
    modes_over_rows((total * weights)[:, None, :] * read, step, filt_ref)
    long_out = (local + filt_ref[...]).astype(BF16)
    gated_b = (queries_b * long_out.astype(F32)).astype(BF16)
    pb_ref[...] = dot(gated_b, out_b[...]).astype(BF16)


def solution(mesh):
    n = mesh.shape["seq"]
    assert n % QUAD == 0

    def on_device(*args):
        rows, width = args[0].shape
        modes = args[9].shape[0]
        args = [a[None] if a.ndim == 1 else a for a in args] + dft_tables(rows)
        block = jax.ShapeDtypeStruct((rows, width), BF16)
        span = sum(size(a) for a in args) + (n + 8) * modes * width * 2
        fast = pltpu.VMEM((rows, width), BF16)
        inside = pl.BlockSpec(memory_space=pltpu.VMEM)
        anywhere = pl.BlockSpec(memory_space=pl.ANY)
        results = pl.pallas_call(
            functools.partial(kernel, n),
            out_shape=(fast, fast),
            in_specs=[anywhere] * len(args),
            out_specs=(inside, inside),
            scratch_shapes=[pltpu.VMEM(a.shape, a.dtype) for a in args]
            + [
                pltpu.VMEM((rows, width), BF16),
                pltpu.VMEM((rows, width), BF16),
                pltpu.VMEM((rows, width), F32),
                pltpu.VMEM((rows, width), BF16),
                pltpu.VMEM((rows, width), BF16),
                pltpu.VMEM((modes, width), F32),
                pltpu.VMEM((modes, width), F32),
                pltpu.VMEM((modes, width), BF16),
                pltpu.VMEM((n // QUAD, modes, width), BF16),
                pltpu.VMEM((n // QUAD, modes, width), BF16),
                pltpu.VMEM((modes, width), F32),
                pltpu.VMEM((span // (4 * LANES), 1, LANES), F32),
                pltpu.SemaphoreType.DMA((4,)),
                pltpu.SemaphoreType.DMA,
                pltpu.SemaphoreType.DMA((PIECES,)),
                pltpu.SemaphoreType.DMA,
                pltpu.SemaphoreType.DMA((2,)),
                pltpu.SemaphoreType.REGULAR,
            ],
            compiler_params=pltpu.CompilerParams(collective_id=0, has_side_effects=True),
        )(*args)
        return pl.pallas_call(
            hand_out,
            out_shape=(block, block),
            in_specs=[inside] * 2,
            out_specs=(anywhere, anywhere),
            scratch_shapes=[
                pltpu.VMEM((2 * rows * width * 2 // (4 * LANES), 1, LANES), F32),
                pltpu.SemaphoreType.DMA,
            ],
        )(*[pltpu.with_memory_space_constraint(r, pltpu.VMEM) for r in results])

    shard = P(("groups", "seq"))
    wide = P(("groups", "seq"), None)
    placed = (wide, shard, P(), P(), P(), P(), shard, P(), P(), P(), P(), P())
    return jax.shard_map(
        on_device, mesh=mesh, in_specs=placed, out_specs=(wide, wide), check_vma=False
    )
```

time: 10.3 us -> 9.89 us (0.960)
  Pallas kernels: 9.52 us -> 9.06 us
    pallas_call x1, Pallas kernels: 8.85 us -> 8.4 us  [on_device(): pl.pallas_call(functools.partial(kernel, n), out_shape=(fast, fast), in_s...]
where the time goes in v3:
time: 9.89 us; the launch traced here: 9.71 us
  Pallas kernels  9.06 us (92%)
  between operations  0.64 us (6%)
    pallas_call x1, Pallas kernels, on_device(): pl.pallas_call(functools.partial(kernel, n), out_shape=(fast, fast), in_s...  8.4 us
    pallas_call x1, Pallas kernels, on_device(): pl.pallas_call(hand_out, out_shape=(block, block), in_specs=[inside] * 2,...  0.66 us

profile of v3, /device:TPU:28, one launch (start us, length us, event | category | flops | bytes accessed | tf_op | source)
XLA Modules:
  0.0 9.7 jit_solution(794550899443516672)
XLA Ops:
  0.6 8.4 %shard_map.158 = (bf16[128,256]{1,0:T(8,128)(2,1)S(1)}, bf16[128,256]{1,0:T(8,128)(2,1)S(1)}) custom-call(bf16[128,256]{1,0:T(8,128)(2,1)} %refs_0_.1, f32[1,128]{1,0:T(1,128)} %bitcast.6, f32[1,256]{1,0:T(1,128)} %bitcast.4, bf16[256,768]{1,0:T(8,128)(2,1)} %refs_3_.1, bf16[128,256]{1,0:T(8,128)(2,1)} %refs_4_.1, bf16[256,256]{1,0:T(8,128)(2,1)} %refs_5_.1, ...), custom_call_target="tpu_custom_call" | custom-call | tf_op jit(solution)/shard_map/pallas_call | solution.py:425
  9.0 0.7 %shard_map.159 = (bf16[128,256]{1,0:T(8,128)(2,1)}, bf16[128,256]{1,0:T(8,128)(2,1)}) custom-call(bf16[128,256]{1,0:T(8,128)(2,1)S(1)} %get-tuple-element.4.a_ref, bf16[128,256]{1,0:T(8,128)(2,1)S(1)} %get-tuple-element.5.b_ref), custom_call_target="tpu_custom_call" | custom-call | tf_op jit(solution)/shard_map/pallas_call | solution.py:453

commit v4 on v3

--- a/solution.py
+++ b/solution.py
@@ -15,6 +15,8 @@
 LANES = 128
 QUAD = 4
 PIECES = 2
+FRONT_PLAN = [(None, 0), (3, 0), (1, 0), (2, 0), (0, 0), (None, 1), (3, 1), (1, 1), (2, 1), (0, 1)]
+REAR_PLAN = [(None, 0), (None, 1), (1, 1), (1, 0), (0, 0), (0, 1), (3, 1), (3, 0), (2, 1), (2, 0)]
 
 
 def dft_tables(rows):
@@ -141,7 +143,9 @@
     vm = refs[17:32]
     (tail_ref, rim_ref, filt_ref, signal_ref, gated_ref) = refs[32:37]
     (own_ref, mate_ref, pair_ref, front_ref, rear_ref, extra_ref, span_ref) = refs[37:44]
-    (load_sem, send_sem, rim_recv, mate_recv, far_recv, far_sem) = refs[44:]
+    (queries_ref, short_ref, base_ref, through_ref, local_ref) = refs[44:49]
+    (load_sem, rim_recv, mate_recv, far_recv, far_sem) = refs[49:]
+    send_sem = load_sem.at[2]
     rows, width = vm[0].shape
     modes = vm[9].shape[0]
 
@@ -215,8 +219,9 @@
 
         @pl.loop(0, level)
         def _(i):
-            signal(far_sem, i * QUAD + (i == 0).astype(jnp.int32))
-            signal(far_sem, i * QUAD + 2)
+            credit = far_sem.at[(level == levels - 1).astype(jnp.int32)]
+            signal(credit, i * QUAD + 2)
+            signal(credit, i * QUAD + (i == 0).astype(jnp.int32))
 
     arrive(0)
     normed = scaled(tok[...], column(rms_a[...]), gain_a[...])
@@ -251,8 +256,8 @@
             copy.start()
 
     arrive(3)
-    queries = dot(normed, proj_a[:, :width])
-    short_own = dot(back_f[...], spectral_product(dot(own_f[...], product), taps_spec))
+    queries_ref[...] = dot(normed, proj_a[:, :width])
+    short_ref[...] = dot(back_f[...], spectral_product(dot(own_f[...], product), taps_spec))
 
     rates = rates_ref[...]
     length = float(n * rows)
@@ -262,17 +267,17 @@
     last = jnp.exp(-rates3 * (SUB - 1.0 - within))
     block = jnp.exp(-rates * float(rows))
     scale_b = column(rms_b[...])
-    base_b = dot(scaled(tok[...], scale_b, gain_b[...]), proj_b[...])
+    base_ref[...] = dot(scaled(tok[...], scale_b, gain_b[...]), proj_b[...])
     high, low = split(out_a[...].astype(F32) * gain_b[...])
-    through = (dot(high, proj_b[...]) + dot(low, proj_b[...])).astype(BF16)
+    through_ref[...] = (dot(high, proj_b[...]) + dot(low, proj_b[...])).astype(BF16)
 
     totals = None
     for i, p in enumerate(pieces):
         rim_copies[i].wait_recv()
         span = slice(i * piece, (i + 1) * piece)
-        gated = (queries[span] * (short_own[span] + rim_ref[p].astype(F32))).astype(BF16)
+        gated = (queries_ref[p] * (short_ref[p] + rim_ref[p].astype(F32))).astype(BF16)
         gated_ref[p] = gated
-        pair_b = base_b[span, width:] + scale_b[span] * dot(gated, through[:, width:])
+        pair_b = base_ref[p, width:] + scale_b[span] * dot(gated, through_ref[:, width:])
         signal = (pair_b[:, :width] * pair_b[:, width:]).astype(BF16)
         signal_ref[p] = signal
         totals = end_totals(totals, signal.astype(F32), step)
@@ -310,28 +315,39 @@
         for i in (1, 0):
             far_copy(front_ref, base + 2 + i, level).start()
 
-    @pl.when(jnp.logical_and(speaks, level < levels - 1))
-    def _():
-        pl.semaphore_wait(far_sem, levels - 1 - level)
-
-    def spread(slots, seats):
-        for seat_there, outward in seats:
-            @pl.loop(0, levels - 1 - level)
-            def _(i):
-                there = level + 1 + i if outward else levels - 1 - i
-                target = there * QUAD + seat_there
-                far_copy(slots, target, there).start()
+    def spread(slots, plan):
+        for seat_there, last_level in plan:
+            if seat_there is None:
+
+                @pl.when(level < levels - (1 if last_level else 2))
+                def _():
+                    if last_level:
+                        pl.semaphore_wait(far_sem.at[1], 1)
+                    else:
+                        pl.semaphore_wait(far_sem.at[0], levels - 2 - level)
+
+            elif last_level:
+
+                @pl.when(level < levels - 1)
+                def _():
+                    far_copy(slots, (levels - 1) * QUAD + seat_there, levels - 1).start()
+
+            else:
+
+                @pl.loop(level + 1, levels - 1)
+                def _(there):
+                    far_copy(slots, there * QUAD + seat_there, there).start()
 
     @pl.when(front)
     def _():
-        spread(front_ref, ((1, False), (0, False), (3, False), (2, False)))
+        spread(front_ref, FRONT_PLAN)
 
     @pl.when(rear)
     def _():
-        spread(rear_ref, ((1, False), (0, True), (3, False), (2, False)))
+        spread(rear_ref, REAR_PLAN)
 
     pa_ref[...] = dot(gated_ref[...], out_a[...]).astype(BF16)
-    queries_b = base_b[:, :width] + scale_b * dot(gated_ref[...], through[:, :width])
+    queries_ref[...] = base_ref[:, :width] + scale_b * dot(gated_ref[...], through_ref[:, :width])
     length = float(n * rows)
     weights = resid_ref[...] * jnp.sqrt(
         one_minus_exp(2.0 * rates) / one_minus_exp(2.0 * rates * length)
@@ -343,7 +359,7 @@
     two_blocks = jnp.exp(-rates * float(2 * rows))
     four_blocks = jnp.exp(-rates * float(4 * rows))
     seated = jnp.exp(-rates * (place * rows).astype(F32))
-    local = dot(back_f[...], spectral_product(dot(own_f[...], signal_ref[...]), long_spec))
+    local_ref[...] = dot(back_f[...], spectral_product(dot(own_f[...], signal_ref[...]), long_spec))
 
     extra_ref[...] = jnp.where(place == 0, jnp.zeros_like(state), mate_ref[...])
 
@@ -404,8 +420,8 @@
 
     total = total * seated + extra_ref[...]
     modes_over_rows((total * weights)[:, None, :] * read, step, filt_ref)
-    long_out = (local + filt_ref[...]).astype(BF16)
-    gated_b = (queries_b * long_out.astype(F32)).astype(BF16)
+    long_out = (local_ref[...] + filt_ref[...]).astype(BF16)
+    gated_b = (queries_ref[...] * long_out.astype(F32)).astype(BF16)
     pb_ref[...] = dot(gated_b, out_b[...]).astype(BF16)
 
 
@@ -441,12 +457,16 @@
                 pltpu.VMEM((n // QUAD, modes, width), BF16),
                 pltpu.VMEM((modes, width), F32),
                 pltpu.VMEM((span // (4 * LANES), 1, LANES), F32),
+                pltpu.VMEM((rows, width), F32),
+                pltpu.VMEM((rows, width), F32),
+                pltpu.VMEM((rows, 3 * width), F32),
+                pltpu.VMEM((width, 3 * width), BF16),
+                pltpu.VMEM((rows, width), F32),
                 pltpu.SemaphoreType.DMA((4,)),
-                pltpu.SemaphoreType.DMA,
                 pltpu.SemaphoreType.DMA((PIECES,)),
                 pltpu.SemaphoreType.DMA,
                 pltpu.SemaphoreType.DMA((2,)),
-                pltpu.SemaphoreType.REGULAR,
+                pltpu.SemaphoreType.REGULAR((2,)),
             ],
             compiler_params=pltpu.CompilerParams(collective_id=0, has_side_effects=True),
         )(*args)

time: 9.89 us -> 9.71 us (0.982)
  Pallas kernels: 9.06 us -> 8.92 us
    pallas_call x1, Pallas kernels: 8.4 us -> 8.26 us  [on_device(): pl.pallas_call(functools.partial(kernel, n), out_shape=(fast, fast), in_s...]
where the time goes in v4:
time: 9.71 us; the launch traced here: 9.57 us
  Pallas kernels  8.92 us (92%)
  between operations  0.64 us (7%)
    pallas_call x1, Pallas kernels, on_device(): pl.pallas_call(functools.partial(kernel, n), out_shape=(fast, fast), in_s...  8.26 us
    pallas_call x1, Pallas kernels, on_device(): pl.pallas_call(hand_out, out_shape=(block, block), in_specs=[inside] * 2,...  0.66 us

profile of v4, /device:TPU:28, one launch (start us, length us, event | category | flops | bytes accessed | tf_op | source)
XLA Modules:
  0.0 9.6 jit_solution(8014125614654012762)
XLA Ops:
  0.6 8.3 %shard_map.158 = (bf16[128,256]{1,0:T(8,128)(2,1)S(1)}, bf16[128,256]{1,0:T(8,128)(2,1)S(1)}) custom-call(bf16[128,256]{1,0:T(8,128)(2,1)} %refs_0_.1, f32[1,128]{1,0:T(1,128)} %bitcast.6, f32[1,256]{1,0:T(1,128)} %bitcast.4, bf16[256,768]{1,0:T(8,128)(2,1)} %refs_3_.1, bf16[128,256]{1,0:T(8,128)(2,1)} %refs_4_.1, bf16[256,256]{1,0:T(8,128)(2,1)} %refs_5_.1, ...), custom_call_target="tpu_custom_call" | custom-call | tf_op jit(solution)/shard_map/pallas_call | solution.py:441
  8.9 0.7 %shard_map.159 = (bf16[128,256]{1,0:T(8,128)(2,1)}, bf16[128,256]{1,0:T(8,128)(2,1)}) custom-call(bf16[128,256]{1,0:T(8,128)(2,1)S(1)} %get-tuple-element.4.a_ref, bf16[128,256]{1,0:T(8,128)(2,1)S(1)} %get-tuple-element.5.b_ref), custom_call_target="tpu_custom_call" | custom-call | tf_op jit(solution)/shard_map/pallas_call | solution.py:473

commit v5 on v4

--- a/solution.py
+++ b/solution.py
@@ -142,9 +142,9 @@
     pa_ref, pb_ref = refs[15:17]
     vm = refs[17:32]
     (tail_ref, rim_ref, filt_ref, signal_ref, gated_ref) = refs[32:37]
-    (own_ref, mate_ref, pair_ref, front_ref, rear_ref, extra_ref, span_ref) = refs[37:44]
-    (queries_ref, short_ref, base_ref, through_ref, local_ref) = refs[44:49]
-    (load_sem, rim_recv, mate_recv, far_recv, far_sem) = refs[49:]
+    (own_ref, mate_ref, pair_ref, front_ref, rear_ref, span_ref) = refs[37:43]
+    (queries_ref, short_ref, base_ref, through_ref, local_ref) = refs[43:48]
+    (load_sem, rim_recv, mate_recv, far_recv, far_sem) = refs[48:]
     send_sem = load_sem.at[2]
     rows, width = vm[0].shape
     modes = vm[9].shape[0]
@@ -310,11 +310,6 @@
         jnp.where(early, state, mate_ref[...]) * block + jnp.where(early, mate_ref[...], state)
     ).astype(BF16)
 
-    @pl.when(front)
-    def _():
-        for i in (1, 0):
-            far_copy(front_ref, base + 2 + i, level).start()
-
     def spread(slots, plan):
         for seat_there, last_level in plan:
             if seat_there is None:
@@ -341,6 +336,8 @@
     @pl.when(front)
     def _():
         spread(front_ref, FRONT_PLAN)
+        for i in (1, 0):
+            far_copy(front_ref, base + 2 + i, level).start()
 
     @pl.when(rear)
     def _():
@@ -361,8 +358,6 @@
     seated = jnp.exp(-rates * (place * rows).astype(F32))
     local_ref[...] = dot(back_f[...], spectral_product(dot(own_f[...], signal_ref[...]), long_spec))
 
-    extra_ref[...] = jnp.where(place == 0, jnp.zeros_like(state), mate_ref[...])
-
     always = size(rim_ref) + size(own_ref)
     letter = size(pair_ref)
 
@@ -411,14 +406,11 @@
     def _():
         settle(span_ref, far_recv.at[1], letter)
 
-    total = lax.fori_loop(older, level, gather, total)
-
-    @pl.when(place >= 2)
-    def _():
-        pairs = front_ref[level].astype(F32)
-        extra_ref[...] = jnp.where(place == 2, pairs, pairs * block + extra_ref[...])
-
-    total = total * seated + extra_ref[...]
+    total = jnp.where(level > 0, gather(older, total), 0.0) * seated
+    pairs = front_ref[level].astype(F32)
+    extra = jnp.where(place == 0, 0.0, mate_ref[...])
+    extra = jnp.where(place < 2, extra, jnp.where(place == 2, pairs, pairs * block + extra))
+    total = total + extra
     modes_over_rows((total * weights)[:, None, :] * read, step, filt_ref)
     long_out = (local_ref[...] + filt_ref[...]).astype(BF16)
     gated_b = (queries_ref[...] * long_out.astype(F32)).astype(BF16)
@@ -455,7 +447,6 @@
                 pltpu.VMEM((modes, width), BF16),
                 pltpu.VMEM((n // QUAD, modes, width), BF16),
                 pltpu.VMEM((n // QUAD, modes, width), BF16),
-                pltpu.VMEM((modes, width), F32),
                 pltpu.VMEM((span // (4 * LANES), 1, LANES), F32),
                 pltpu.VMEM((rows, width), F32),
                 pltpu.VMEM((rows, width), F32),

time: 9.71 us -> 9.71 us (level)
  no operation moved by 1% of the time
where the time goes in v5:
time: 9.71 us; the launch traced here: 9.56 us
  Pallas kernels  8.92 us (92%)
  between operations  0.64 us (7%)
    pallas_call x1, Pallas kernels, on_device(): pl.pallas_call(functools.partial(kernel, n), out_shape=(fast, fast), in_s...  8.26 us
    pallas_call x1, Pallas kernels, on_device(): pl.pallas_call(hand_out, out_shape=(block, block), in_specs=[inside] * 2,...  0.66 us

profile of v5, /device:TPU:28, one launch (start us, length us, event | category | flops | bytes accessed | tf_op | source)
XLA Modules:
  0.0 9.6 jit_solution(14054937794986574293)
XLA Ops:
  0.6 8.3 %shard_map.158 = (bf16[128,256]{1,0:T(8,128)(2,1)S(1)}, bf16[128,256]{1,0:T(8,128)(2,1)S(1)}) custom-call(bf16[128,256]{1,0:T(8,128)(2,1)} %refs_0_.1, f32[1,128]{1,0:T(1,128)} %bitcast.6, f32[1,256]{1,0:T(1,128)} %bitcast.4, bf16[256,768]{1,0:T(8,128)(2,1)} %refs_3_.1, bf16[128,256]{1,0:T(8,128)(2,1)} %refs_4_.1, bf16[256,256]{1,0:T(8,128)(2,1)} %refs_5_.1, ...), custom_call_target="tpu_custom_call" | custom-call | tf_op jit(solution)/shard_map/pallas_call | solution.py:433
  8.9 0.7 %shard_map.159 = (bf16[128,256]{1,0:T(8,128)(2,1)}, bf16[128,256]{1,0:T(8,128)(2,1)}) custom-call(bf16[128,256]{1,0:T(8,128)(2,1)S(1)} %get-tuple-element.4.a_ref, bf16[128,256]{1,0:T(8,128)(2,1)S(1)} %get-tuple-element.5.b_ref), custom_call_target="tpu_custom_call" | custom-call | tf_op jit(solution)/shard_map/pallas_call | solution.py:464

commit v6 on v5

--- a/solution.py
+++ b/solution.py
@@ -198,12 +198,13 @@
         def _(i):
             signal(barrier, i * QUAD + 2)
 
-    start(2, 3)
+    start(2)
     (tok, rms_a, gain_a, proj_a, taps, out_a) = vm[:6]
     (rms_b, gain_b, proj_b, rates_ref, resid_ref, out_b, own_f, rim_f, back_f) = vm[6:]
 
-    piece = rows // PIECES
-    pieces = [pl.ds(p * piece, piece) for p in range(PIECES)]
+    cut = rows * 5 // 8
+    spans = ((0, cut), (cut, rows))
+    pieces = [pl.ds(a, b - a) for a, b in spans]
 
     @pl.when(me == 0)
     def _():
@@ -226,6 +227,7 @@
     arrive(0)
     normed = scaled(tok[...], column(rms_a[...]), gain_a[...])
     arrive(1)
+    start(3)
     pair_a = dot(normed, proj_a[:, width:])
     product = (pair_a[:, :width] * pair_a[:, width:]).astype(BF16)
     arrive(2)
@@ -274,7 +276,7 @@
     totals = None
     for i, p in enumerate(pieces):
         rim_copies[i].wait_recv()
-        span = slice(i * piece, (i + 1) * piece)
+        span = slice(*spans[i])
         gated = (queries_ref[p] * (short_ref[p] + rim_ref[p].astype(F32))).astype(BF16)
         gated_ref[p] = gated
         pair_b = base_ref[p, width:] + scale_b[span] * dot(gated, through_ref[:, width:])

time: 9.71 us -> 9.72 us (level)
  no operation moved by 1% of the time
where the time goes in v6:
time: 9.72 us; the launch traced here: 9.57 us
  Pallas kernels  8.93 us (92%)
  between operations  0.64 us (7%)
    pallas_call x1, Pallas kernels, on_device(): pl.pallas_call(functools.partial(kernel, n), out_shape=(fast, fast), in_s...  8.27 us
    pallas_call x1, Pallas kernels, on_device(): pl.pallas_call(hand_out, out_shape=(block, block), in_specs=[inside] * 2,...  0.66 us

profile of v6, /device:TPU:28, one launch (start us, length us, event | category | flops | bytes accessed | tf_op | source)
XLA Modules:
  0.0 9.6 jit_solution(6029580743394452287)
XLA Ops:
  0.6 8.3 %shard_map.158 = (bf16[128,256]{1,0:T(8,128)(2,1)S(1)}, bf16[128,256]{1,0:T(8,128)(2,1)S(1)}) custom-call(bf16[128,256]{1,0:T(8,128)(2,1)} %refs_0_.1, f32[1,128]{1,0:T(1,128)} %bitcast.6, f32[1,256]{1,0:T(1,128)} %bitcast.4, bf16[256,768]{1,0:T(8,128)(2,1)} %refs_3_.1, bf16[128,256]{1,0:T(8,128)(2,1)} %refs_4_.1, bf16[256,256]{1,0:T(8,128)(2,1)} %refs_5_.1, ...), custom_call_target="tpu_custom_call" | custom-call | tf_op jit(solution)/shard_map/pallas_call | solution.py:435
  8.9 0.7 %shard_map.159 = (bf16[128,256]{1,0:T(8,128)(2,1)}, bf16[128,256]{1,0:T(8,128)(2,1)}) custom-call(bf16[128,256]{1,0:T(8,128)(2,1)S(1)} %get-tuple-element.4.a_ref, bf16[128,256]{1,0:T(8,128)(2,1)S(1)} %get-tuple-element.5.b_ref), custom_call_target="tpu_custom_call" | custom-call | tf_op jit(solution)/shard_map/pallas_call | solution.py:466

commit v7 on v6

--- a/solution.py
+++ b/solution.py
@@ -188,8 +188,7 @@
     def _():
         signal(barrier, me - 1)
 
-    @pl.loop(1, QUAD)
-    def _(i):
+    for i in range(1, QUAD):
         signal(barrier, base + lax.rem(place + QUAD - i, QUAD))
 
     @pl.when(speaks)

time: 9.72 us -> 9.72 us (level)
  no operation moved by 1% of the time
where the time goes in v7:
time: 9.72 us; the launch traced here: 9.57 us
  Pallas kernels  8.93 us (92%)
  between operations  0.64 us (7%)
    pallas_call x1, Pallas kernels, on_device(): pl.pallas_call(functools.partial(kernel, n), out_shape=(fast, fast), in_s...  8.27 us
    pallas_call x1, Pallas kernels, on_device(): pl.pallas_call(hand_out, out_shape=(block, block), in_specs=[inside] * 2,...  0.66 us

profile of v7, /device:TPU:28, one launch (start us, length us, event | category | flops | bytes accessed | tf_op | source)
XLA Modules:
  0.0 9.6 jit_solution(6420492470400716924)
XLA Ops:
  0.6 8.3 %shard_map.158 = (bf16[128,256]{1,0:T(8,128)(2,1)S(1)}, bf16[128,256]{1,0:T(8,128)(2,1)S(1)}) custom-call(bf16[128,256]{1,0:T(8,128)(2,1)} %refs_0_.1, f32[1,128]{1,0:T(1,128)} %bitcast.6, f32[1,256]{1,0:T(1,128)} %bitcast.4, bf16[256,768]{1,0:T(8,128)(2,1)} %refs_3_.1, bf16[128,256]{1,0:T(8,128)(2,1)} %refs_4_.1, bf16[256,256]{1,0:T(8,128)(2,1)} %refs_5_.1, ...), custom_call_target="tpu_custom_call" | custom-call | tf_op jit(solution)/shard_map/pallas_call | solution.py:434
  8.9 0.7 %shard_map.159 = (bf16[128,256]{1,0:T(8,128)(2,1)}, bf16[128,256]{1,0:T(8,128)(2,1)}) custom-call(bf16[128,256]{1,0:T(8,128)(2,1)S(1)} %get-tuple-element.4.a_ref, bf16[128,256]{1,0:T(8,128)(2,1)S(1)} %get-tuple-element.5.b_ref), custom_call_target="tpu_custom_call" | custom-call | tf_op jit(solution)/shard_map/pallas_call | solution.py:465
